TPU v7x, 32 devices: a whole 2x2x4 slice. The times are simulated.
32 devices in a mesh: group: 2 (over y), expert: 16 (over z, x, core), token: 1.
Axes of the slice: x: 2, y: 2, z: 4, core: 2. Of those that a mesh axis runs over, the one named last changes fastest.
Arguments:
- tokens: bfloat16 [4096, 2048], P(('group', 'expert', 'token')), parts along dimension 0, may hold values from -6 to 6
- expert_ids: int32 [4096, 8], P(('group', 'expert', 'token')), parts along dimension 0, may hold values from 0 to 15, all different within a row; in each aligned block of 128 rows (0 to 127, 128 to 255, ...) at most 96 rows name the same one
- route_weights: float32 [4096, 8], P(('group', 'expert', 'token')), parts along dimension 0, may hold values from 0.05 to 1
- gate_up: bfloat16 [16, 2048, 768], P('expert', 'token'), may hold values from -0.125 to 0.125
- down_t: bfloat16 [16, 2048, 384], P('expert', 'token'), may hold values from -0.3125 to 0.3125
Outputs:
- moe_out: bfloat16 [4096, 2048], P(('group', 'expert', 'token')), parts along dimension 0
There are 2 independent parts, one for each index of `group`. A program takes and returns all parts, laid end to end along the dimension named above; an argument that names none is the same for every part. Nothing has to cross between parts.
Inputs may be any that keep to these rules, and one draw needn't show every extreme that they name: `expert_ids`: each row names 8 different experts. Within the rows of one device (aligned blocks of 128 rows) no expert is named by more than 96 rows, a bound that some block reaches.
All inputs are finite; a program needn't handle non-finite values.
Results may differ from a plain program's by a relative error of at most 0.0058.
Values may be sent and summed in bfloat16 or wider, within the bound.
No kernel may reach another device: no remote copies, remote signals or barrier semaphores. Data moves between devices by JAX's collectives and lax.ppermute only.
A program may use at most 128 MiB of HBM per device.

v0:
```python
import functools

import jax
import jax.numpy as jnp
from jax import lax
from jax.experimental import pallas as pl
from jax.experimental.pallas import tpu as pltpu
from jax.sharding import PartitionSpec as P


def expert_apply(arrived, full_gate_up, full_down):
    shape = arrived.shape
    width = full_down.shape[2]
    rows = arrived.reshape(-1, shape[-1])
    pre = jnp.dot(rows, full_gate_up[0], preferred_element_type=jnp.float32)
    hidden = (jax.nn.silu(pre[:, :width]) * pre[:, width:]).astype(jnp.bfloat16)
    outputs = lax.dot_general(
        hidden, full_down[0], (((1,), (1,)), ((), ())), preferred_element_type=jnp.float32
    )
    return outputs.astype(jnp.bfloat16).reshape(shape)


def exchange_rows(tokens, expert_ids, route_weights, gate_up, down_t):
    tok_rows, choices_each = expert_ids.shape
    features = tokens.shape[1]
    num_experts = lax.axis_size("expert")
    slot_count = min(
        tok_rows, (3 * tok_rows * choices_each + 2 * num_experts - 1) // (2 * num_experts)
    )
    full_gate_up, full_down = (
        lax.all_gather(gate_up, "token", axis=1, tiled=True),
        lax.all_gather(down_t, "token", axis=1, tiled=True),
    )
    flat_ids = expert_ids.reshape(-1)
    onehot = (flat_ids[:, None] == jnp.arange(num_experts, dtype=jnp.int32)[None, :]).astype(
        jnp.int32
    )
    running = jnp.cumsum(onehot, axis=0)
    ranks = jnp.sum(running * onehot, axis=1) - 1
    slots = flat_ids * slot_count + ranks
    repeated = jnp.repeat(tokens, choices_each, axis=0)
    outgoing = jnp.zeros((num_experts * slot_count, features), jnp.bfloat16).at[slots].set(repeated)
    outgoing = outgoing.reshape(num_experts, slot_count, features)
    arrived = lax.all_to_all(outgoing, "expert", split_axis=0, concat_axis=0, tiled=True)
    served = expert_apply(arrived, full_gate_up, full_down)
    returned = lax.all_to_all(served, "expert", split_axis=0, concat_axis=0, tiled=True)
    picked = returned.reshape(num_experts * slot_count, features)[slots]
    picked = picked.reshape(tok_rows, choices_each, features)
    total = jnp.zeros((tok_rows, features), jnp.float32)
    for which in range(choices_each):
        total = total + route_weights[:, which : which + 1] * picked[:, which].astype(jnp.float32)
    return total.astype(jnp.bfloat16)


def chip_cycle(mesh):
    devices = mesh.devices[0, :, 0]
    chips = {}
    for index, device in enumerate(devices):
        chips.setdefault(tuple(getattr(device, "coords", (index // 2,))), []).append(index)
    coords = sorted(chips)
    wide = [d for d in range(len(coords[0])) if len({c[d] for c in coords}) > 1]
    if len(wide) == 2:
        wide.sort(key=lambda d: len({c[d] for c in coords}))
        short, long = wide
        turn = {v: i for i, v in enumerate(sorted({c[short] for c in coords}))}
        coords.sort(key=lambda c: (turn[c[short]], c[long] if turn[c[short]] % 2 == 0 else -c[long]))
    return [chips[c] for c in coords]


LANES = 128


def pack_rows(num_experts, *refs):
    far, outs, near, done = refs[:3], refs[3:5], refs[5:8], refs[8]
    copies = [pltpu.make_async_copy(a, b, done.at[i]) for i, (a, b) in enumerate(zip(far, near))]
    for copy in copies:
        copy.start()
    for copy in copies:
        copy.wait()
    tokens, ids, weights = near
    tok_rows, features = tokens.shape
    half = features // 2
    for start in range(0, features, LANES):
        at = start % half // LANES * tok_rows
        outs[start // half][at : at + tok_rows] = tokens[:, start : start + LANES]
    place = lax.broadcasted_iota(jnp.int32, (num_experts, tok_rows), 0)
    share = jnp.zeros(place.shape, jnp.float32)
    for choice in range(ids.shape[0]):
        named = ids[choice : choice + 1] == place
        share += jnp.where(named, weights[choice : choice + 1], 0.0)
    high = share.astype(jnp.bfloat16).astype(jnp.float32)
    both = jnp.concatenate([high, share - high], axis=0)
    outs[1][half // LANES * tok_rows :] = both.astype(jnp.bfloat16)


def serve_rows(width, picks, partner, *refs):
    pieces, refs, out = refs[: -1 - 2 * len(picks)], refs[-1 - 2 * len(picks) : -1], refs[-1]
    tok_rows, _ = out.shape
    num_experts = len(partner)
    rows = [
        piece[at : at + tok_rows]
        for piece in pieces
        for at in range(0, piece.shape[0] - tok_rows + 1, tok_rows)
    ]
    rows = jnp.concatenate(rows, axis=1)
    shares = jnp.transpose(pieces[-1][-2 * num_experts :].astype(jnp.float32))
    lanes = lax.broadcasted_iota(jnp.int32, shares.shape, 1)
    me = lax.axis_index("expert")
    other = sum(jnp.where(me == e, partner[e], 0) for e in range(num_experts))
    total = None
    for place, which in enumerate(picks):
        gate, down = refs[2 * place], refs[2 * place + 1]
        expert = (me, other)[which]
        share = jnp.where((lanes == expert) | (lanes == expert + num_experts), shares, 0.0)
        share = jnp.sum(share, axis=1, keepdims=True)
        pre = jnp.dot(rows, gate[...], preferred_element_type=jnp.float32)
        gated, up = pre[:, :width], pre[:, width:]
        hidden = gated / (1.0 + jnp.exp(-gated)) * up * share
        part = lax.dot_general(
            hidden.astype(jnp.bfloat16),
            down[...],
            (((1,), (1,)), ((), ())),
            preferred_element_type=jnp.float32,
        )
        total = part if total is None else total + part
    out[...] = total


def ring(stops, tokens, expert_ids, route_weights, gate_up, down_t):
    tok_rows, features = tokens.shape
    num_experts, width = lax.axis_size("expert"), down_t.shape[2]
    count = len(stops)
    partner = [0] * num_experts
    onward = [0] * num_experts
    for s in range(count):
        for place, turn in ((0, 1), (1, -1)):
            partner[stops[s][place]] = stops[s][1 - place]
            onward[stops[s][place]] = stops[(s + turn) % count][place]
    hop = functools.partial(lax.ppermute, axis_name="expert", perm=list(enumerate(onward)))
    swap = functools.partial(lax.ppermute, axis_name="expert", perm=list(enumerate(partner)))
    whole = pl.BlockSpec(memory_space=pltpu.VMEM)

    given = (tokens, expert_ids.T, route_weights.T)
    given = [pltpu.with_memory_space_constraint(x, pltpu.HBM) for x in given]
    half = features // 2 // LANES * tok_rows
    packed = pl.pallas_call(
        functools.partial(pack_rows, num_experts),
        out_shape=[
            jax.ShapeDtypeStruct((rows, LANES), jnp.bfloat16)
            for rows in (half, half + 2 * num_experts)
        ],
        in_specs=[pl.BlockSpec(memory_space=pltpu.HBM)] * 3,
        out_specs=[whole] * 2,
        scratch_shapes=[pltpu.VMEM(x.shape, x.dtype) for x in given]
        + [pltpu.SemaphoreType.DMA((3,))],
        compiler_params=pltpu.CompilerParams(vmem_limit_bytes=8 * 1024 * 1024),
        name="pack_rows",
    )(*given)
    away = [hop(x) for x in packed]
    weights = [(gate_up[0], down_t[0])]
    weights.append(tuple(swap(w) for w in weights[0]))

    def serve(pieces, picks):
        return pl.pallas_call(
            functools.partial(serve_rows, width, picks, partner),
            out_shape=jax.ShapeDtypeStruct((tok_rows, features), jnp.float32),
            in_specs=[whole] * (len(pieces) + 2 * len(picks)),
            out_specs=whole,
            compiler_params=pltpu.CompilerParams(vmem_limit_bytes=8 * 1024 * 1024),
            name="serve_rows",
        )(*pieces, *(w for which in picks for w in weights[which]))

    def after(arrays, other):
        return [lax.optimization_barrier((x, other))[0] for x in arrays]

    home = serve(packed, (0,))
    away = after(away, home)
    total = None
    for step in range(1, count):
        here = away
        if step < count - 1:
            away = [hop(x) for x in (away if step == 1 else [jnp.concatenate(away)])]
        more = serve(here, (0, 1))
        away = after(away, more)
        parts = 2 if step >= count - 2 else 1
        more = jnp.split(more, parts)
        if total is not None:
            if len(total) < parts:
                total = jnp.split(total[0], parts)
        sent = []
        for at, x in enumerate(more):
            if total is not None:
                y = after([total[at]], sent)[0] if parts > 1 else total[at]
                x = x + y.astype(jnp.float32)
            sent.append(x.astype(jnp.bfloat16))
        total = []
        for x in sent:
            total.append(hop(x))
    home += serve(packed, (1,))
    return (home + jnp.concatenate(total).astype(jnp.float32)).astype(jnp.bfloat16)


def solution(mesh):
    placed = (
        P(("group", "expert", "token"), None),
        P(("group", "expert", "token"), None),
        P(("group", "expert", "token"), None),
        P("expert", "token", None),
        P("expert", "token", None),
    )

    stops = chip_cycle(mesh)
    cycle = mesh.shape["token"] == 1 and {len(s) for s in stops} == {2} and len(stops) > 2

    def per_device(tokens, expert_ids, route_weights, gate_up, down_t):
        fits = cycle and mesh.shape["expert"] <= 4 * expert_ids.shape[1] and gate_up.shape[0] == 1
        if fits and tokens.shape[0] == LANES and tokens.shape[1] % (2 * LANES) == 0:
            return ring(stops, tokens, expert_ids, route_weights, gate_up, down_t)
        return exchange_rows(tokens, expert_ids, route_weights, gate_up, down_t)

    return jax.shard_map(
        per_device,
        mesh=mesh,
        in_specs=placed,
        out_specs=P(("group", "expert", "token"), None),
        check_vma=False,
    )
```

profile of v0, /device:TPU:0, one launch (start us, length us, event | category | flops | bytes accessed | tf_op | source)
XLA Modules:
  0.0 92.8 jit_solution(12910942721008173547)
XLA Ops:
  0.0 0.5 collective-permute-start
  0.5 1.2 %pack_rows.1 = (bf16[1024,128]{1,0:T(8,128)(2,1)S(1)}, bf16[1056,128]{1,0:T(8,128)(2,1)S(1)}) custom-call(bf16[128,2048]{1,0:T(8,128)(2,1)} %refs_0_.1, s32[8,128]{1,0:T(8,128)} %bitcast.22, f32[8,128]{1,0:T(8,128)} %bitcast.23), custom_call_target="tpu_custom_call" | custom-call | tf_op jit(solution)/shard_map/pack_rows/pallas_call | solution.py:146
  1.7 3.1 %collective-permute-start.4 = (bf16[1056,128]{1,0:T(8,128)(2,1)S(1)}, bf16[1056,128]{1,0:T(8,128)(2,1)S(1)}, u32[]{:S(2)}, u32[]{:S(2)}) collective-permute-start(bf16[1056,128]{1,0:T(8,128)(2,1)S(1)} %get-tuple-element.19.refs_1_), channel_id=1, source_target_pairs={{0,4},{1,3},{2,0},{3,7},{4,8},{5,1},{6,2},{7,11},{8,12},{9,5},{10,... | collective-permute-start | bytes 811016 | tf_op jit(solution)/shard_map/ppermute | solution.py:159
  4.8 1.6 %collective-permute-start.2 = (bf16[1024,128]{1,0:T(8,128)(2,1)S(1)}, bf16[1024,128]{1,0:T(8,128)(2,1)S(1)}, u32[]{:S(2)}, u32[]{:S(2)}) collective-permute-start(bf16[1024,128]{1,0:T(8,128)(2,1)S(1)} %get-tuple-element.18.refs_0_), channel_id=1, source_target_pairs={{0,4},{1,3},{2,0},{3,7},{4,8},{5,1},{6,2},{7,11},{8,12},{9,5},{10,... | collective-permute-start | bytes 786440 | tf_op jit(solution)/shard_map/ppermute | solution.py:159
  6.4 1.9 %copy-done = bf16[1,2048,768]{2,1,0:T(8,128)(2,1)S(1)} copy-done((bf16[1,2048,768]{2,1,0:T(8,128)(2,1)S(1)}, bf16[1,2048,768]{2,1,0:T(8,128)(2,1)}, u32[]{:S(2)}) %copy-start) | copy-done | bytes 3145752
  8.3 1.4 %copy-done.2 = bf16[1,2048,384]{2,1,0:T(8,128)(2,1)S(1)} copy-done((bf16[1,2048,384]{2,1,0:T(8,128)(2,1)S(1)}, bf16[1,2048,384]{2,1,0:T(8,128)(2,1)}, u32[]{:S(2)}) %copy-start.2) | copy-done | bytes 1572888
  9.7 1.3 %serve_rows.9 = f32[128,2048]{1,0:T(8,128)S(1)} custom-call(bf16[1024,128]{1,0:T(8,128)(2,1)S(1)} %get-tuple-element.18.refs_0_, bf16[1056,128]{1,0:T(8,128)(2,1)S(1)} %get-tuple-element.19.refs_1_, bf16[2048,768]{1,0:T(8,128)(2,1)S(1)} %bitcast.5, bf16[2048,384]{1,0:T(8,128)(2,1)S(1)} %bitcast.14), custom_call_target="tpu_custom_call" | custom-call | tf_op jit(solution)/shard_map/serve_rows/pallas_call | solution.py:164
  11.0 1.6 %collective-permute-start.5 = (bf16[1056,128]{1,0:T(8,128)(2,1)S(1)}, bf16[1056,128]{1,0:T(8,128)(2,1)S(1)}, u32[]{:S(2)}, u32[]{:S(2)}) collective-permute-start(bf16[1056,128]{1,0:T(8,128)(2,1)S(1)} %collective-permute-done.4.refs_1_), channel_id=1, source_target_pairs={{0,4},{1,3},{2,0},{3,7},{4,8},{5,1},{6,2},{7,11},{8,12},{9,5},{10,... | collective-permute-start | bytes 811016 | tf_op jit(solution)/shard_map/ppermute | solution.py:182
  12.6 1.5 %collective-permute-start.3 = (bf16[1024,128]{1,0:T(8,128)(2,1)S(1)}, bf16[1024,128]{1,0:T(8,128)(2,1)S(1)}, u32[]{:S(2)}, u32[]{:S(2)}) collective-permute-start(bf16[1024,128]{1,0:T(8,128)(2,1)S(1)} %collective-permute-done.2.refs_0_), channel_id=1, source_target_pairs={{0,4},{1,3},{2,0},{3,7},{4,8},{5,1},{6,2},{7,11},{8,12},{9,5},{10,... | collective-permute-start | bytes 786440 | tf_op jit(solution)/shard_map/ppermute | solution.py:182
  14.2 2.0 %serve_rows.11 = f32[128,2048]{1,0:T(8,128)S(1)} custom-call(bf16[1024,128]{1,0:T(8,128)(2,1)S(1)} %collective-permute-done.2.refs_0_, bf16[1056,128]{1,0:T(8,128)(2,1)S(1)} %collective-permute-done.4.refs_1_, bf16[2048,768]{1,0:T(8,128)(2,1)S(1)} %bitcast.6, bf16[2048,384]{1,0:T(8,128)(2,1)S(1)} %bitcast.15, ...), custom_call_target="tpu_custom_call" | custom-call | tf_op jit(solution)/shard_map/serve_rows/pallas_call | solution.py:164
  16.3 1.6 %collective-permute-start.11 = (bf16[128,2048]{1,0:T(8,128)(2,1)S(1)}, bf16[128,2048]{1,0:T(8,128)(2,1)S(1)}, u32[]{:S(2)}, u32[]{:S(2)}) collective-permute-start(bf16[128,2048]{1,0:T(8,128)(2,1)S(1)} %convert_element_type.57), channel_id=1, source_target_pairs={{0,4},{1,3},{2,0},{3,7},{4,8},{5,1},{6,2},{7,11},{8,12},{9,5},{10,... | collective-permute-start | bytes 1572872 | tf_op jit(solution)/shard_map/ppermute | solution.py:198
  17.8 2.5 %collective-permute-done.3.refs_0_ = bf16[1024,128]{1,0:T(8,128)(2,1)S(1)} collective-permute-done((bf16[1024,128]{1,0:T(8,128)(2,1)S(1)}, bf16[1024,128]{1,0:T(8,128)(2,1)S(1)}, u32[]{:S(2)}, u32[]{:S(2)}) %collective-permute-start.3) | collective-permute-done | bytes 262176 | tf_op jit(solution)/shard_map/ppermute | solution.py:182
  20.4 1.6 %collective-permute-start.6 = (bf16[2080,128]{1,0:T(8,128)(2,1)S(1)}, bf16[2080,128]{1,0:T(8,128)(2,1)S(1)}, u32[]{:S(2)}, u32[]{:S(2)}) collective-permute-start(bf16[2080,128]{1,0:T(8,128)(2,1)S(1)} %pad_maximum_fusion), channel_id=1, source_target_pairs={{0,4},{1,3},{2,0},{3,7},{4,8},{5,1},{6,2},{7,11},{8,12},{9,5},{10,... | collective-permute-start | bytes 1597448 | tf_op jit(solution)/shard_map/ppermute | solution.py:182
  22.0 2.0 %serve_rows.12 = f32[128,2048]{1,0:T(8,128)S(1)} custom-call(bf16[1024,128]{1,0:T(8,128)(2,1)S(1)} %collective-permute-done.3.refs_0_, bf16[1056,128]{1,0:T(8,128)(2,1)S(1)} %collective-permute-done.5.refs_1_, bf16[2048,768]{1,0:T(8,128)(2,1)S(1)} %bitcast.7, bf16[2048,384]{1,0:T(8,128)(2,1)S(1)} %bitcast.16, ...), custom_call_target="tpu_custom_call" | custom-call | tf_op jit(solution)/shard_map/serve_rows/pallas_call | solution.py:164
  24.0 1.9 %collective-permute-done.11 = bf16[128,2048]{1,0:T(8,128)(2,1)S(1)} collective-permute-done((bf16[128,2048]{1,0:T(8,128)(2,1)S(1)}, bf16[128,2048]{1,0:T(8,128)(2,1)S(1)}, u32[]{:S(2)}, u32[]{:S(2)}) %collective-permute-start.11) | collective-permute-done | bytes 524320 | tf_op jit(solution)/shard_map/ppermute | solution.py:198
  26.1 1.6 %collective-permute-start.12 = (bf16[128,2048]{1,0:T(8,128)(2,1)S(1)}, bf16[128,2048]{1,0:T(8,128)(2,1)S(1)}, u32[]{:S(2)}, u32[]{:S(2)}) collective-permute-start(bf16[128,2048]{1,0:T(8,128)(2,1)S(1)} %add_convert_fusion.4), channel_id=1, source_target_pairs={{0,4},{1,3},{2,0},{3,7},{4,8},{5,1},{6,2},{7,11},{8,12},{9,5},{10,... | collective-permute-start | bytes 1572872 | tf_op jit(solution)/shard_map/ppermute | solution.py:198
  27.7 4.0 %collective-permute-done.6.refs_0_ = bf16[2080,128]{1,0:T(8,128)(2,1)S(1)} collective-permute-done((bf16[2080,128]{1,0:T(8,128)(2,1)S(1)}, bf16[2080,128]{1,0:T(8,128)(2,1)S(1)}, u32[]{:S(2)}, u32[]{:S(2)}) %collective-permute-start.6) | collective-permute-done | bytes 532512 | tf_op jit(solution)/shard_map/ppermute | solution.py:182
  31.7 1.6 %collective-permute-start.7 = (bf16[2080,128]{1,0:T(8,128)(2,1)S(1)}, bf16[2080,128]{1,0:T(8,128)(2,1)S(1)}, u32[]{:S(2)}, u32[]{:S(2)}) collective-permute-start(bf16[2080,128]{1,0:T(8,128)(2,1)S(1)} %collective-permute-done.6.refs_0_), channel_id=1, source_target_pairs={{0,4},{1,3},{2,0},{3,7},{4,8},{5,1},{6,2},{7,11},{8,12},{9,5},{10,... | collective-permute-start | bytes 1597448 | tf_op jit(solution)/shard_map/ppermute | solution.py:182
  33.2 2.0 %serve_rows.13 = f32[128,2048]{1,0:T(8,128)S(1)} custom-call(bf16[2080,128]{1,0:T(8,128)(2,1)S(1)} %collective-permute-done.6.refs_0_, bf16[2048,768]{1,0:T(8,128)(2,1)S(1)} %bitcast.8, bf16[2048,384]{1,0:T(8,128)(2,1)S(1)} %bitcast.17, bf16[2048,768]{1,0:T(8,128)(2,1)S(1)} %collective-permute-done.refs_2_.refs_4_.refs_3_, ...), custom_call_target="tpu_custom_call" | custom-call | tf_op jit(solution)/shard_map/serve_rows/pallas_call | solution.py:164
  35.2 2.0 %collective-permute-done.12 = bf16[128,2048]{1,0:T(8,128)(2,1)S(1)} collective-permute-done((bf16[128,2048]{1,0:T(8,128)(2,1)S(1)}, bf16[128,2048]{1,0:T(8,128)(2,1)S(1)}, u32[]{:S(2)}, u32[]{:S(2)}) %collective-permute-start.12) | collective-permute-done | bytes 524320 | tf_op jit(solution)/shard_map/ppermute | solution.py:198
  37.4 1.6 %collective-permute-start.13 = (bf16[128,2048]{1,0:T(8,128)(2,1)S(1)}, bf16[128,2048]{1,0:T(8,128)(2,1)S(1)}, u32[]{:S(2)}, u32[]{:S(2)}) collective-permute-start(bf16[128,2048]{1,0:T(8,128)(2,1)S(1)} %add_convert_fusion.3), channel_id=1, source_target_pairs={{0,4},{1,3},{2,0},{3,7},{4,8},{5,1},{6,2},{7,11},{8,12},{9,5},{10,... | collective-permute-start | bytes 1572872 | tf_op jit(solution)/shard_map/ppermute | solution.py:198
  39.0 4.0 %collective-permute-done.7.refs_0_ = bf16[2080,128]{1,0:T(8,128)(2,1)S(1)} collective-permute-done((bf16[2080,128]{1,0:T(8,128)(2,1)S(1)}, bf16[2080,128]{1,0:T(8,128)(2,1)S(1)}, u32[]{:S(2)}, u32[]{:S(2)}) %collective-permute-start.7) | collective-permute-done | bytes 532512 | tf_op jit(solution)/shard_map/ppermute | solution.py:182
  43.0 1.6 %collective-permute-start.8 = (bf16[2080,128]{1,0:T(8,128)(2,1)S(1)}, bf16[2080,128]{1,0:T(8,128)(2,1)S(1)}, u32[]{:S(2)}, u32[]{:S(2)}) collective-permute-start(bf16[2080,128]{1,0:T(8,128)(2,1)S(1)} %collective-permute-done.7.refs_0_), channel_id=1, source_target_pairs={{0,4},{1,3},{2,0},{3,7},{4,8},{5,1},{6,2},{7,11},{8,12},{9,5},{10,... | collective-permute-start | bytes 1597448 | tf_op jit(solution)/shard_map/ppermute | solution.py:182
  44.6 2.1 %serve_rows.14 = f32[128,2048]{1,0:T(8,128)S(1)} custom-call(bf16[2080,128]{1,0:T(8,128)(2,1)S(1)} %collective-permute-done.7.refs_0_, bf16[2048,768]{1,0:T(8,128)(2,1)S(1)} %bitcast.9, bf16[2048,384]{1,0:T(8,128)(2,1)S(1)} %bitcast.18, bf16[2048,768]{1,0:T(8,128)(2,1)S(1)} %collective-permute-done.refs_2_.refs_4_.refs_3_, ...), custom_call_target="tpu_custom_call" | custom-call | tf_op jit(solution)/shard_map/serve_rows/pallas_call | solution.py:164
  46.6 2.0 %collective-permute-done.13 = bf16[128,2048]{1,0:T(8,128)(2,1)S(1)} collective-permute-done((bf16[128,2048]{1,0:T(8,128)(2,1)S(1)}, bf16[128,2048]{1,0:T(8,128)(2,1)S(1)}, u32[]{:S(2)}, u32[]{:S(2)}) %collective-permute-start.13) | collective-permute-done | bytes 524320 | tf_op jit(solution)/shard_map/ppermute | solution.py:198
  48.6 0.1 add_convert_fusion.2
  48.7 1.6 %collective-permute-start.14 = (bf16[128,2048]{1,0:T(8,128)(2,1)S(1)}, bf16[128,2048]{1,0:T(8,128)(2,1)S(1)}, u32[]{:S(2)}, u32[]{:S(2)}) collective-permute-start(bf16[128,2048]{1,0:T(8,128)(2,1)S(1)} %add_convert_fusion.2), channel_id=1, source_target_pairs={{0,4},{1,3},{2,0},{3,7},{4,8},{5,1},{6,2},{7,11},{8,12},{9,5},{10,... | collective-permute-start | bytes 1572872 | tf_op jit(solution)/shard_map/ppermute | solution.py:198
  50.4 3.9 %collective-permute-done.8.refs_0_ = bf16[2080,128]{1,0:T(8,128)(2,1)S(1)} collective-permute-done((bf16[2080,128]{1,0:T(8,128)(2,1)S(1)}, bf16[2080,128]{1,0:T(8,128)(2,1)S(1)}, u32[]{:S(2)}, u32[]{:S(2)}) %collective-permute-start.8) | collective-permute-done | bytes 532512 | tf_op jit(solution)/shard_map/ppermute | solution.py:182
  54.3 1.6 %collective-permute-start.9 = (bf16[2080,128]{1,0:T(8,128)(2,1)S(1)}, bf16[2080,128]{1,0:T(8,128)(2,1)S(1)}, u32[]{:S(2)}, u32[]{:S(2)}) collective-permute-start(bf16[2080,128]{1,0:T(8,128)(2,1)S(1)} %collective-permute-done.8.refs_0_), channel_id=1, source_target_pairs={{0,4},{1,3},{2,0},{3,7},{4,8},{5,1},{6,2},{7,11},{8,12},{9,5},{10,... | collective-permute-start | bytes 1597448 | tf_op jit(solution)/shard_map/ppermute | solution.py:182
  55.9 2.0 %serve_rows.15 = f32[128,2048]{1,0:T(8,128)S(1)} custom-call(bf16[2080,128]{1,0:T(8,128)(2,1)S(1)} %collective-permute-done.8.refs_0_, bf16[2048,768]{1,0:T(8,128)(2,1)S(1)} %bitcast.10, bf16[2048,384]{1,0:T(8,128)(2,1)S(1)} %bitcast.19, bf16[2048,768]{1,0:T(8,128)(2,1)S(1)} %collective-permute-done.refs_2_.refs_4_.refs_3_, ...), custom_call_target="tpu_custom_call" | custom-call | tf_op jit(solution)/shard_map/serve_rows/pallas_call | solution.py:164
  57.9 2.0 %collective-permute-done.14 = bf16[128,2048]{1,0:T(8,128)(2,1)S(1)} collective-permute-done((bf16[128,2048]{1,0:T(8,128)(2,1)S(1)}, bf16[128,2048]{1,0:T(8,128)(2,1)S(1)}, u32[]{:S(2)}, u32[]{:S(2)}) %collective-permute-start.14) | collective-permute-done | bytes 524320 | tf_op jit(solution)/shard_map/ppermute | solution.py:198
  60.1 1.6 %collective-permute-start.15 = (bf16[128,2048]{1,0:T(8,128)(2,1)S(1)}, bf16[128,2048]{1,0:T(8,128)(2,1)S(1)}, u32[]{:S(2)}, u32[]{:S(2)}) collective-permute-start(bf16[128,2048]{1,0:T(8,128)(2,1)S(1)} %add_convert_fusion.1), channel_id=1, source_target_pairs={{0,4},{1,3},{2,0},{3,7},{4,8},{5,1},{6,2},{7,11},{8,12},{9,5},{10,... | collective-permute-start | bytes 1572872 | tf_op jit(solution)/shard_map/ppermute | solution.py:198
  61.7 3.9 %collective-permute-done.9.refs_0_ = bf16[2080,128]{1,0:T(8,128)(2,1)S(1)} collective-permute-done((bf16[2080,128]{1,0:T(8,128)(2,1)S(1)}, bf16[2080,128]{1,0:T(8,128)(2,1)S(1)}, u32[]{:S(2)}, u32[]{:S(2)}) %collective-permute-start.9) | collective-permute-done | bytes 532512 | tf_op jit(solution)/shard_map/ppermute | solution.py:182
  65.6 1.6 %collective-permute-start.10 = (bf16[2080,128]{1,0:T(8,128)(2,1)S(1)}, bf16[2080,128]{1,0:T(8,128)(2,1)S(1)}, u32[]{:S(2)}, u32[]{:S(2)}) collective-permute-start(bf16[2080,128]{1,0:T(8,128)(2,1)S(1)} %collective-permute-done.9.refs_0_), channel_id=1, source_target_pairs={{0,4},{1,3},{2,0},{3,7},{4,8},{5,1},{6,2},{7,11},{8,12},{9,5},{10,... | collective-permute-start | bytes 1597448 | tf_op jit(solution)/shard_map/ppermute | solution.py:182
  67.2 2.0 %serve_rows.16 = f32[128,2048]{1,0:T(8,128)S(1)} custom-call(bf16[2080,128]{1,0:T(8,128)(2,1)S(1)} %collective-permute-done.9.refs_0_, bf16[2048,768]{1,0:T(8,128)(2,1)S(1)} %bitcast.11, bf16[2048,384]{1,0:T(8,128)(2,1)S(1)} %bitcast.20, bf16[2048,768]{1,0:T(8,128)(2,1)S(1)} %collective-permute-done.refs_2_.refs_4_.refs_3_, ...), custom_call_target="tpu_custom_call" | custom-call | tf_op jit(solution)/shard_map/serve_rows/pallas_call | solution.py:164
  69.2 2.0 %collective-permute-done.15 = bf16[128,2048]{1,0:T(8,128)(2,1)S(1)} collective-permute-done((bf16[128,2048]{1,0:T(8,128)(2,1)S(1)}, bf16[128,2048]{1,0:T(8,128)(2,1)S(1)}, u32[]{:S(2)}, u32[]{:S(2)}) %collective-permute-start.15) | collective-permute-done | bytes 524320 | tf_op jit(solution)/shard_map/ppermute | solution.py:198
  71.3 1.6 %collective-permute-start.16 = (bf16[64,2048]{1,0:T(8,128)(2,1)S(1)}, bf16[64,2048]{1,0:T(8,128)(2,1)S(1)}, u32[]{:S(2)}, u32[]{:S(2)}) collective-permute-start(bf16[64,2048]{1,0:T(8,128)(2,1)S(1)} %fusion.2), channel_id=1, source_target_pairs={{0,4},{1,3},{2,0},{3,7},{4,8},{5,1},{6,2},{7,11},{8,12},{9,5},{10,... | collective-permute-start | bytes 786440 | tf_op jit(solution)/shard_map/ppermute | solution.py:198
  73.0 1.5 %collective-permute-start.18 = (bf16[64,2048]{1,0:T(8,128)(2,1)S(1)}, bf16[64,2048]{1,0:T(8,128)(2,1)S(1)}, u32[]{:S(2)}, u32[]{:S(2)}) collective-permute-start(bf16[64,2048]{1,0:T(8,128)(2,1)S(1)} %fusion), channel_id=1, source_target_pairs={{0,4},{1,3},{2,0},{3,7},{4,8},{5,1},{6,2},{7,11},{8,12},{9,5},{10,... | collective-permute-start | bytes 786440 | tf_op jit(solution)/shard_map/ppermute | solution.py:198
  74.6 2.4 %collective-permute-done.10.refs_0_ = bf16[2080,128]{1,0:T(8,128)(2,1)S(1)} collective-permute-done((bf16[2080,128]{1,0:T(8,128)(2,1)S(1)}, bf16[2080,128]{1,0:T(8,128)(2,1)S(1)}, u32[]{:S(2)}, u32[]{:S(2)}) %collective-permute-start.10) | collective-permute-done | bytes 532512 | tf_op jit(solution)/shard_map/ppermute | solution.py:182
  76.9 2.1 %serve_rows.17 = f32[128,2048]{1,0:T(8,128)S(1)} custom-call(bf16[2080,128]{1,0:T(8,128)(2,1)S(1)} %collective-permute-done.10.refs_0_, bf16[2048,768]{1,0:T(8,128)(2,1)S(1)} %bitcast.12, bf16[2048,384]{1,0:T(8,128)(2,1)S(1)} %bitcast.21, bf16[2048,768]{1,0:T(8,128)(2,1)S(1)} %collective-permute-done.refs_2_.refs_4_.refs_3_, ...), custom_call_target="tpu_custom_call" | custom-call | tf_op jit(solution)/shard_map/serve_rows/pallas_call | solution.py:164
  79.0 0.7 collective-permute-done.16
  79.8 2.8 %collective-permute-done.18 = bf16[64,2048]{1,0:T(8,128)(2,1)S(1)} collective-permute-done((bf16[64,2048]{1,0:T(8,128)(2,1)S(1)}, bf16[64,2048]{1,0:T(8,128)(2,1)S(1)}, u32[]{:S(2)}, u32[]{:S(2)}) %collective-permute-start.18) | collective-permute-done | bytes 262176 | tf_op jit(solution)/shard_map/ppermute | solution.py:198
  82.6 1.6 %collective-permute-start.19 = (bf16[64,2048]{1,0:T(8,128)(2,1)S(1)}, bf16[64,2048]{1,0:T(8,128)(2,1)S(1)}, u32[]{:S(2)}, u32[]{:S(2)}) collective-permute-start(bf16[64,2048]{1,0:T(8,128)(2,1)S(1)} %fusion.1), channel_id=1, source_target_pairs={{0,4},{1,3},{2,0},{3,7},{4,8},{5,1},{6,2},{7,11},{8,12},{9,5},{10,... | collective-permute-start | bytes 786440 | tf_op jit(solution)/shard_map/ppermute | solution.py:198
  84.2 1.5 %collective-permute-start.17 = (bf16[64,2048]{1,0:T(8,128)(2,1)S(1)}, bf16[64,2048]{1,0:T(8,128)(2,1)S(1)}, u32[]{:S(2)}, u32[]{:S(2)}) collective-permute-start(bf16[64,2048]{1,0:T(8,128)(2,1)S(1)} %fusion.3), channel_id=1, source_target_pairs={{0,4},{1,3},{2,0},{3,7},{4,8},{5,1},{6,2},{7,11},{8,12},{9,5},{10,... | collective-permute-start | bytes 786440 | tf_op jit(solution)/shard_map/ppermute | solution.py:198
  85.7 1.3 %serve_rows.10 = f32[128,2048]{1,0:T(8,128)S(1)} custom-call(bf16[1024,128]{1,0:T(8,128)(2,1)S(1)} %get-tuple-element.18.refs_0_, bf16[1056,128]{1,0:T(8,128)(2,1)S(1)} %get-tuple-element.19.refs_1_, bf16[2048,768]{1,0:T(8,128)(2,1)S(1)} %collective-permute-done.refs_2_.refs_4_.refs_3_, bf16[2048,384]{1,0:T(8,128)(2,1)S(1)} %collective-permute-done.1.refs_3_.refs_5_.refs_4_), custom_call_target="tpu_custom_call" | custom-call | tf_op jit(solution)/shard_map/serve_rows/pallas_call | solution.py:164
  87.1 2.0 %collective-permute-done.19 = bf16[64,2048]{1,0:T(8,128)(2,1)S(1)} collective-permute-done((bf16[64,2048]{1,0:T(8,128)(2,1)S(1)}, bf16[64,2048]{1,0:T(8,128)(2,1)S(1)}, u32[]{:S(2)}, u32[]{:S(2)}) %collective-permute-start.19) | collective-permute-done | bytes 262176 | tf_op jit(solution)/shard_map/ppermute | solution.py:198
  89.0 2.8 %collective-permute-done.17 = bf16[64,2048]{1,0:T(8,128)(2,1)S(1)} collective-permute-done((bf16[64,2048]{1,0:T(8,128)(2,1)S(1)}, bf16[64,2048]{1,0:T(8,128)(2,1)S(1)}, u32[]{:S(2)}, u32[]{:S(2)}) %collective-permute-start.17) | collective-permute-done | bytes 262176 | tf_op jit(solution)/shard_map/ppermute | solution.py:198
  91.9 1.0 %add_convert_fusion = bf16[128,2048]{1,0:T(8,128)(2,1)} fusion(f32[128,2048]{1,0:T(8,128)S(1)} %serve_rows.9, f32[128,2048]{1,0:T(8,128)S(1)} %serve_rows.10, bf16[64,2048]{1,0:T(8,128)(2,1)S(1)} %collective-permute-done.19, bf16[64,2048]{1,0:T(8,128)(2,1)S(1)} %collective-permute-done.17), kind=kLoop, calls=%fused_computation | loop fusion | flops 1835008 | bytes 3145728 | tf_op jit(solution)/shard_map/convert_element_type | solution.py:200
  (22 shorter events, 0.7 us)
Async XLA Ops:
  0.0 14.1 %collective-permute-start = (bf16[2048,768]{1,0:T(8,128)(2,1)}, bf16[2048,768]{1,0:T(8,128)(2,1)S(1)}, u32[]{:S(2)}, u32[]{:S(2)}) collective-permute-start(bf16[2048,768]{1,0:T(8,128)(2,1)} %bitcast.4), channel_id=1, source_target_pairs={{0,1},{1,0},{2,3},{3,2},{4,5},{5,4},{6,7},{7,6},{8,9},{9,8},{10,11... | collective-permute-start | bytes 9437192 | tf_op jit(solution)/shard_map/ppermute | solution.py:161
  0.5 13.6 %collective-permute-start.1 = (bf16[2048,384]{1,0:T(8,128)(2,1)}, bf16[2048,384]{1,0:T(8,128)(2,1)S(1)}, u32[]{:S(2)}, u32[]{:S(2)}) collective-permute-start(bf16[2048,384]{1,0:T(8,128)(2,1)} %bitcast.13), channel_id=1, source_target_pairs={{0,1},{1,0},{2,3},{3,2},{4,5},{5,4},{6,7},{7,6},{8,9},{9,8},{10,11... | collective-permute-start | bytes 4718600 | tf_op jit(solution)/shard_map/ppermute | solution.py:161
  1.7 9.3 %collective-permute-start.4 = (bf16[1056,128]{1,0:T(8,128)(2,1)S(1)}, bf16[1056,128]{1,0:T(8,128)(2,1)S(1)}, u32[]{:S(2)}, u32[]{:S(2)}) collective-permute-start(bf16[1056,128]{1,0:T(8,128)(2,1)S(1)} %get-tuple-element.19.refs_1_), channel_id=1, source_target_pairs={{0,4},{1,3},{2,0},{3,7},{4,8},{5,1},{6,2},{7,11},{8,12},{9,5},{10,... | collective-permute-start | bytes 811016 | tf_op jit(solution)/shard_map/ppermute | solution.py:159
  4.8 7.8 %collective-permute-start.2 = (bf16[1024,128]{1,0:T(8,128)(2,1)S(1)}, bf16[1024,128]{1,0:T(8,128)(2,1)S(1)}, u32[]{:S(2)}, u32[]{:S(2)}) collective-permute-start(bf16[1024,128]{1,0:T(8,128)(2,1)S(1)} %get-tuple-element.18.refs_0_), channel_id=1, source_target_pairs={{0,4},{1,3},{2,0},{3,7},{4,8},{5,1},{6,2},{7,11},{8,12},{9,5},{10,... | collective-permute-start | bytes 786440 | tf_op jit(solution)/shard_map/ppermute | solution.py:159
  6.4 1.9 %copy-start = (bf16[1,2048,768]{2,1,0:T(8,128)(2,1)S(1)}, bf16[1,2048,768]{2,1,0:T(8,128)(2,1)}, u32[]{:S(2)}) copy-start(bf16[1,2048,768]{2,1,0:T(8,128)(2,1)} %param.8) | copy-start | bytes 9437188
  8.3 1.4 %copy-start.2 = (bf16[1,2048,384]{2,1,0:T(8,128)(2,1)S(1)}, bf16[1,2048,384]{2,1,0:T(8,128)(2,1)}, u32[]{:S(2)}) copy-start(bf16[1,2048,384]{2,1,0:T(8,128)(2,1)} %param.9) | copy-start | bytes 4718596
  9.7 4.5 %copy-start.1 = (bf16[1,2048,768]{2,1,0:T(8,128)(2,1)S(1)}, bf16[1,2048,768]{2,1,0:T(8,128)(2,1)}, u32[]{:S(2)}) copy-start(bf16[1,2048,768]{2,1,0:T(8,128)(2,1)} %param.8) | copy-start | bytes 9437188
  11.0 6.8 %collective-permute-start.5 = (bf16[1056,128]{1,0:T(8,128)(2,1)S(1)}, bf16[1056,128]{1,0:T(8,128)(2,1)S(1)}, u32[]{:S(2)}, u32[]{:S(2)}) collective-permute-start(bf16[1056,128]{1,0:T(8,128)(2,1)S(1)} %collective-permute-done.4.refs_1_), channel_id=1, source_target_pairs={{0,4},{1,3},{2,0},{3,7},{4,8},{5,1},{6,2},{7,11},{8,12},{9,5},{10,... | collective-permute-start | bytes 811016 | tf_op jit(solution)/shard_map/ppermute | solution.py:182
  12.6 7.7 %collective-permute-start.3 = (bf16[1024,128]{1,0:T(8,128)(2,1)S(1)}, bf16[1024,128]{1,0:T(8,128)(2,1)S(1)}, u32[]{:S(2)}, u32[]{:S(2)}) collective-permute-start(bf16[1024,128]{1,0:T(8,128)(2,1)S(1)} %collective-permute-done.2.refs_0_), channel_id=1, source_target_pairs={{0,4},{1,3},{2,0},{3,7},{4,8},{5,1},{6,2},{7,11},{8,12},{9,5},{10,... | collective-permute-start | bytes 786440 | tf_op jit(solution)/shard_map/ppermute | solution.py:182
  16.2 5.8 %copy-start.3 = (bf16[1,2048,384]{2,1,0:T(8,128)(2,1)S(1)}, bf16[1,2048,384]{2,1,0:T(8,128)(2,1)}, u32[]{:S(2)}) copy-start(bf16[1,2048,384]{2,1,0:T(8,128)(2,1)} %param.9) | copy-start | bytes 4718596
  16.3 9.7 %collective-permute-start.11 = (bf16[128,2048]{1,0:T(8,128)(2,1)S(1)}, bf16[128,2048]{1,0:T(8,128)(2,1)S(1)}, u32[]{:S(2)}, u32[]{:S(2)}) collective-permute-start(bf16[128,2048]{1,0:T(8,128)(2,1)S(1)} %convert_element_type.57), channel_id=1, source_target_pairs={{0,4},{1,3},{2,0},{3,7},{4,8},{5,1},{6,2},{7,11},{8,12},{9,5},{10,... | collective-permute-start | bytes 1572872 | tf_op jit(solution)/shard_map/ppermute | solution.py:198
  20.4 11.3 %collective-permute-start.6 = (bf16[2080,128]{1,0:T(8,128)(2,1)S(1)}, bf16[2080,128]{1,0:T(8,128)(2,1)S(1)}, u32[]{:S(2)}, u32[]{:S(2)}) collective-permute-start(bf16[2080,128]{1,0:T(8,128)(2,1)S(1)} %pad_maximum_fusion), channel_id=1, source_target_pairs={{0,4},{1,3},{2,0},{3,7},{4,8},{5,1},{6,2},{7,11},{8,12},{9,5},{10,... | collective-permute-start | bytes 1597448 | tf_op jit(solution)/shard_map/ppermute | solution.py:182
  26.1 11.2 %collective-permute-start.12 = (bf16[128,2048]{1,0:T(8,128)(2,1)S(1)}, bf16[128,2048]{1,0:T(8,128)(2,1)S(1)}, u32[]{:S(2)}, u32[]{:S(2)}) collective-permute-start(bf16[128,2048]{1,0:T(8,128)(2,1)S(1)} %add_convert_fusion.4), channel_id=1, source_target_pairs={{0,4},{1,3},{2,0},{3,7},{4,8},{5,1},{6,2},{7,11},{8,12},{9,5},{10,... | collective-permute-start | bytes 1572872 | tf_op jit(solution)/shard_map/ppermute | solution.py:198
  31.7 11.3 %collective-permute-start.7 = (bf16[2080,128]{1,0:T(8,128)(2,1)S(1)}, bf16[2080,128]{1,0:T(8,128)(2,1)S(1)}, u32[]{:S(2)}, u32[]{:S(2)}) collective-permute-start(bf16[2080,128]{1,0:T(8,128)(2,1)S(1)} %collective-permute-done.6.refs_0_), channel_id=1, source_target_pairs={{0,4},{1,3},{2,0},{3,7},{4,8},{5,1},{6,2},{7,11},{8,12},{9,5},{10,... | collective-permute-start | bytes 1597448 | tf_op jit(solution)/shard_map/ppermute | solution.py:182
  37.4 11.2 %collective-permute-start.13 = (bf16[128,2048]{1,0:T(8,128)(2,1)S(1)}, bf16[128,2048]{1,0:T(8,128)(2,1)S(1)}, u32[]{:S(2)}, u32[]{:S(2)}) collective-permute-start(bf16[128,2048]{1,0:T(8,128)(2,1)S(1)} %add_convert_fusion.3), channel_id=1, source_target_pairs={{0,4},{1,3},{2,0},{3,7},{4,8},{5,1},{6,2},{7,11},{8,12},{9,5},{10,... | collective-permute-start | bytes 1572872 | tf_op jit(solution)/shard_map/ppermute | solution.py:198
  43.0 11.3 %collective-permute-start.8 = (bf16[2080,128]{1,0:T(8,128)(2,1)S(1)}, bf16[2080,128]{1,0:T(8,128)(2,1)S(1)}, u32[]{:S(2)}, u32[]{:S(2)}) collective-permute-start(bf16[2080,128]{1,0:T(8,128)(2,1)S(1)} %collective-permute-done.7.refs_0_), channel_id=1, source_target_pairs={{0,4},{1,3},{2,0},{3,7},{4,8},{5,1},{6,2},{7,11},{8,12},{9,5},{10,... | collective-permute-start | bytes 1597448 | tf_op jit(solution)/shard_map/ppermute | solution.py:182
  48.7 11.2 %collective-permute-start.14 = (bf16[128,2048]{1,0:T(8,128)(2,1)S(1)}, bf16[128,2048]{1,0:T(8,128)(2,1)S(1)}, u32[]{:S(2)}, u32[]{:S(2)}) collective-permute-start(bf16[128,2048]{1,0:T(8,128)(2,1)S(1)} %add_convert_fusion.2), channel_id=1, source_target_pairs={{0,4},{1,3},{2,0},{3,7},{4,8},{5,1},{6,2},{7,11},{8,12},{9,5},{10,... | collective-permute-start | bytes 1572872 | tf_op jit(solution)/shard_map/ppermute | solution.py:198
  54.3 11.3 %collective-permute-start.9 = (bf16[2080,128]{1,0:T(8,128)(2,1)S(1)}, bf16[2080,128]{1,0:T(8,128)(2,1)S(1)}, u32[]{:S(2)}, u32[]{:S(2)}) collective-permute-start(bf16[2080,128]{1,0:T(8,128)(2,1)S(1)} %collective-permute-done.8.refs_0_), channel_id=1, source_target_pairs={{0,4},{1,3},{2,0},{3,7},{4,8},{5,1},{6,2},{7,11},{8,12},{9,5},{10,... | collective-permute-start | bytes 1597448 | tf_op jit(solution)/shard_map/ppermute | solution.py:182
  60.1 11.2 %collective-permute-start.15 = (bf16[128,2048]{1,0:T(8,128)(2,1)S(1)}, bf16[128,2048]{1,0:T(8,128)(2,1)S(1)}, u32[]{:S(2)}, u32[]{:S(2)}) collective-permute-start(bf16[128,2048]{1,0:T(8,128)(2,1)S(1)} %add_convert_fusion.1), channel_id=1, source_target_pairs={{0,4},{1,3},{2,0},{3,7},{4,8},{5,1},{6,2},{7,11},{8,12},{9,5},{10,... | collective-permute-start | bytes 1572872 | tf_op jit(solution)/shard_map/ppermute | solution.py:198
  65.6 11.3 %collective-permute-start.10 = (bf16[2080,128]{1,0:T(8,128)(2,1)S(1)}, bf16[2080,128]{1,0:T(8,128)(2,1)S(1)}, u32[]{:S(2)}, u32[]{:S(2)}) collective-permute-start(bf16[2080,128]{1,0:T(8,128)(2,1)S(1)} %collective-permute-done.9.refs_0_), channel_id=1, source_target_pairs={{0,4},{1,3},{2,0},{3,7},{4,8},{5,1},{6,2},{7,11},{8,12},{9,5},{10,... | collective-permute-start | bytes 1597448 | tf_op jit(solution)/shard_map/ppermute | solution.py:182
  71.3 8.4 %collective-permute-start.16 = (bf16[64,2048]{1,0:T(8,128)(2,1)S(1)}, bf16[64,2048]{1,0:T(8,128)(2,1)S(1)}, u32[]{:S(2)}, u32[]{:S(2)}) collective-permute-start(bf16[64,2048]{1,0:T(8,128)(2,1)S(1)} %fusion.2), channel_id=1, source_target_pairs={{0,4},{1,3},{2,0},{3,7},{4,8},{5,1},{6,2},{7,11},{8,12},{9,5},{10,... | collective-permute-start | bytes 786440 | tf_op jit(solution)/shard_map/ppermute | solution.py:198
  73.0 9.5 %collective-permute-start.18 = (bf16[64,2048]{1,0:T(8,128)(2,1)S(1)}, bf16[64,2048]{1,0:T(8,128)(2,1)S(1)}, u32[]{:S(2)}, u32[]{:S(2)}) collective-permute-start(bf16[64,2048]{1,0:T(8,128)(2,1)S(1)} %fusion), channel_id=1, source_target_pairs={{0,4},{1,3},{2,0},{3,7},{4,8},{5,1},{6,2},{7,11},{8,12},{9,5},{10,... | collective-permute-start | bytes 786440 | tf_op jit(solution)/shard_map/ppermute | solution.py:198
  82.6 6.4 %collective-permute-start.19 = (bf16[64,2048]{1,0:T(8,128)(2,1)S(1)}, bf16[64,2048]{1,0:T(8,128)(2,1)S(1)}, u32[]{:S(2)}, u32[]{:S(2)}) collective-permute-start(bf16[64,2048]{1,0:T(8,128)(2,1)S(1)} %fusion.1), channel_id=1, source_target_pairs={{0,4},{1,3},{2,0},{3,7},{4,8},{5,1},{6,2},{7,11},{8,12},{9,5},{10,... | collective-permute-start | bytes 786440 | tf_op jit(solution)/shard_map/ppermute | solution.py:198
  84.2 7.6 %collective-permute-start.17 = (bf16[64,2048]{1,0:T(8,128)(2,1)S(1)}, bf16[64,2048]{1,0:T(8,128)(2,1)S(1)}, u32[]{:S(2)}, u32[]{:S(2)}) collective-permute-start(bf16[64,2048]{1,0:T(8,128)(2,1)S(1)} %fusion.3), channel_id=1, source_target_pairs={{0,4},{1,3},{2,0},{3,7},{4,8},{5,1},{6,2},{7,11},{8,12},{9,5},{10,... | collective-permute-start | bytes 786440 | tf_op jit(solution)/shard_map/ppermute | solution.py:198
where the time goes:
time: 93 us; the launch traced here: 92.8 us
  waiting for transfers between devices  39 us (42%)
  starting transfers between devices  30.6 us (33%)
  Pallas kernels  18 us (19%)
  local copies, waits for them, and re-layouts  3.34 us (4%)
  other arithmetic  1.73 us (2%)
    ppermute x7, waiting for transfers between devices, ring(): away = [hop(x) for x in (away if step == 1 else [jnp.concatenate(away)])]  20.7 us
    ppermute x9, waiting for transfers between devices, ring(): total.append(hop(x))  18.3 us
    pallas_call x9, Pallas kernels, serve(): pl.pallas_call(functools.partial(serve_rows, width, picks, partner), out_...  16.8 us
    ppermute x9, starting transfers between devices, ring(): total.append(hop(x))  14.4 us
    ppermute x7, starting transfers between devices, ring(): away = [hop(x) for x in (away if step == 1 else [jnp.concatenate(away)])]  11.1 us
    ppermute x2, starting transfers between devices, ring(): away = [hop(x) for x in packed]  4.68 us
    unnamed x8, local copies, waits for them, and re-layouts  3.31 us
  transfers between devices with their start and end apart: 20, of which 15 were waited for; matrix products, arithmetic and copies ran while one was open for 1% of the time, Pallas kernels for 19%

commit v1 on v0

--- a/solution.py
+++ b/solution.py
@@ -91,6 +91,16 @@
     high = share.astype(jnp.bfloat16).astype(jnp.float32)
     both = jnp.concatenate([high, share - high], axis=0)
     outs[1][half // LANES * tok_rows :] = both.astype(jnp.bfloat16)
+
+
+def load(*refs):
+    count = len(refs) // 2
+    done = refs[-1]
+    copies = [pltpu.make_async_copy(refs[i], refs[count + i], done.at[i]) for i in range(count)]
+    for copy in copies:
+        copy.start()
+    for copy in copies:
+        copy.wait()
 
 
 def serve_rows(width, picks, partner, *refs):
@@ -157,8 +167,18 @@
         name="pack_rows",
     )(*given)
     away = [hop(x) for x in packed]
-    weights = [(gate_up[0], down_t[0])]
-    weights.append(tuple(swap(w) for w in weights[0]))
+    own = (gate_up[0], down_t[0])
+    swapped = [swap(w) for w in own]
+    held = pl.pallas_call(
+        load,
+        out_shape=[jax.ShapeDtypeStruct(w.shape, w.dtype) for w in own],
+        in_specs=[pl.BlockSpec(memory_space=pltpu.HBM)] * 2,
+        out_specs=[whole] * 2,
+        scratch_shapes=[pltpu.SemaphoreType.DMA((2,))],
+        compiler_params=pltpu.CompilerParams(vmem_limit_bytes=2 * 1024 * 1024),
+        name="load",
+    )(*(pltpu.with_memory_space_constraint(w, pltpu.HBM) for w in own))
+    weights = (held, swapped)
 
     def serve(pieces, picks):
         return pl.pallas_call(
@@ -173,13 +193,14 @@
     def after(arrays, other):
         return [lax.optimization_barrier((x, other))[0] for x in arrays]
 
-    home = serve(packed, (0,))
-    away = after(away, home)
+    away = after(away, held)
     total = None
     for step in range(1, count):
-        here = away
+        here = list(away)
         if step < count - 1:
-            away = [hop(x) for x in (away if step == 1 else [jnp.concatenate(away)])]
+            away = away if step == 1 else [jnp.concatenate(away)]
+            for at, x in enumerate(away):
+                away[at] = hop(x)
         more = serve(here, (0, 1))
         away = after(away, more)
         parts = 2 if step >= count - 2 else 1
@@ -196,7 +217,7 @@
         total = []
         for x in sent:
             total.append(hop(x))
-    home += serve(packed, (1,))
+    home = serve(packed, (0, 1))
     return (home + jnp.concatenate(total).astype(jnp.float32)).astype(jnp.bfloat16)
 
 

time: 93 us -> 92.4 us (level)
  local copies, waits for them, and re-layouts: 3.34 us -> 0.04 us
  starting transfers between devices: 30.6 us -> 32.7 us
  Pallas kernels: 18 us -> 19.8 us
  waiting for transfers between devices: 39 us -> 37.9 us
    unnamed x8 -> x0, local copies, waits for them, and re-layouts: 3.31 us -> none
    pallas_call x0 -> x1, Pallas kernels: none -> 2.37 us  [ring(): pl.pallas_call(load, out_shape=[jax.ShapeDtypeStruct(w.shape, w.dtype) fo...]
    ppermute x9, waiting for transfers between devices: 20.7 us -> 18.5 us  [the longest x7 18.5 us: ring(): away[at] = hop(x)]
    ppermute x9, starting transfers between devices: 11.6 us -> 13.2 us  [the longest x7 12.7 us: ring(): away[at] = hop(x)]
    ppermute x2, waiting for transfers between devices: 0.01 us -> 1.1 us  [ring(): away = [hop(x) for x in packed]]
    pallas_call x9 -> x8, Pallas kernels: 16.8 us -> 16.3 us  [serve(): pl.pallas_call(functools.partial(serve_rows, width, picks, partner), out_...]
  transfers between devices with their start and end apart: 20 -> 20, of which waited for: 15 -> 17; matrix products, arithmetic and copies ran while one was open for 1% -> 1% of each run, Pallas kernels for 19% -> 21%
where the time goes in v1:
time: 92.4 us; the launch traced here: 92.3 us
  waiting for transfers between devices  37.9 us (41%)
  starting transfers between devices  32.7 us (35%)
  Pallas kernels  19.8 us (21%)
  other arithmetic  1.68 us (2%)
    ppermute x7, waiting for transfers between devices, ring(): away[at] = hop(x)  18.5 us
    ppermute x9, waiting for transfers between devices, ring(): total.append(hop(x))  18.3 us
    pallas_call x8, Pallas kernels, serve(): pl.pallas_call(functools.partial(serve_rows, width, picks, partner), out_...  16.3 us
    ppermute x9, starting transfers between devices, ring(): total.append(hop(x))  14.8 us
    ppermute x7, starting transfers between devices, ring(): away[at] = hop(x)  12.7 us
    ppermute x2, starting transfers between devices, ring(): away = [hop(x) for x in packed]  4.68 us
    pallas_call x1, Pallas kernels, ring(): pl.pallas_call(load, out_shape=[jax.ShapeDtypeStruct(w.shape, w.dtype) fo...  2.37 us
  transfers between devices with their start and end apart: 20, of which 17 were waited for; matrix products, arithmetic and copies ran while one was open for 1% of the time, Pallas kernels for 21%

profile of v1, /device:TPU:0, one launch (start us, length us, event | category | flops | bytes accessed | tf_op | source)
XLA Modules:
  0.0 92.3 jit_solution(13396585425958020375)
XLA Ops:
  0.0 0.5 collective-permute-start
  0.5 1.2 %pack_rows.1 = (bf16[1024,128]{1,0:T(8,128)(2,1)S(1)}, bf16[1056,128]{1,0:T(8,128)(2,1)S(1)}) custom-call(bf16[128,2048]{1,0:T(8,128)(2,1)} %refs_0_.1, s32[8,128]{1,0:T(8,128)} %bitcast.8, f32[8,128]{1,0:T(8,128)} %bitcast.9), custom_call_target="tpu_custom_call" | custom-call | tf_op jit(solution)/shard_map/pack_rows/pallas_call | solution.py:156
  1.7 3.1 %collective-permute-start.4 = (bf16[1056,128]{1,0:T(8,128)(2,1)S(1)}, bf16[1056,128]{1,0:T(8,128)(2,1)S(1)}, u32[]{:S(2)}, u32[]{:S(2)}) collective-permute-start(bf16[1056,128]{1,0:T(8,128)(2,1)S(1)} %get-tuple-element.21.refs_1_), channel_id=1, source_target_pairs={{0,4},{1,3},{2,0},{3,7},{4,8},{5,1},{6,2},{7,11},{8,12},{9,5},{10,... | collective-permute-start | bytes 811016 | tf_op jit(solution)/shard_map/ppermute | solution.py:169
  4.8 1.6 %collective-permute-start.2 = (bf16[1024,128]{1,0:T(8,128)(2,1)S(1)}, bf16[1024,128]{1,0:T(8,128)(2,1)S(1)}, u32[]{:S(2)}, u32[]{:S(2)}) collective-permute-start(bf16[1024,128]{1,0:T(8,128)(2,1)S(1)} %get-tuple-element.20.refs_0_), channel_id=1, source_target_pairs={{0,4},{1,3},{2,0},{3,7},{4,8},{5,1},{6,2},{7,11},{8,12},{9,5},{10,... | collective-permute-start | bytes 786440 | tf_op jit(solution)/shard_map/ppermute | solution.py:169
  6.4 2.4 %load.1 = (bf16[2048,768]{1,0:T(8,128)(2,1)S(1)}, bf16[2048,384]{1,0:T(8,128)(2,1)S(1)}) custom-call(bf16[2048,768]{1,0:T(8,128)(2,1)} %bitcast.5, bf16[2048,384]{1,0:T(8,128)(2,1)} %bitcast.7), custom_call_target="tpu_custom_call" | custom-call | tf_op jit(solution)/shard_map/load/pallas_call | solution.py:172
  8.8 0.4 collective-permute-done.4.refs_1_
  9.2 2.1 %collective-permute-start.5 = (bf16[1056,128]{1,0:T(8,128)(2,1)S(1)}, bf16[1056,128]{1,0:T(8,128)(2,1)S(1)}, u32[]{:S(2)}, u32[]{:S(2)}) collective-permute-start(bf16[1056,128]{1,0:T(8,128)(2,1)S(1)} %collective-permute-done.4.refs_1_), channel_id=1, source_target_pairs={{0,4},{1,3},{2,0},{3,7},{4,8},{5,1},{6,2},{7,11},{8,12},{9,5},{10,... | collective-permute-start | bytes 811016 | tf_op jit(solution)/shard_map/ppermute | solution.py:203
  11.3 0.7 collective-permute-done.2.refs_0_
  12.0 2.1 %collective-permute-start.3 = (bf16[1024,128]{1,0:T(8,128)(2,1)S(1)}, bf16[1024,128]{1,0:T(8,128)(2,1)S(1)}, u32[]{:S(2)}, u32[]{:S(2)}) collective-permute-start(bf16[1024,128]{1,0:T(8,128)(2,1)S(1)} %collective-permute-done.2.refs_0_), channel_id=1, source_target_pairs={{0,4},{1,3},{2,0},{3,7},{4,8},{5,1},{6,2},{7,11},{8,12},{9,5},{10,... | collective-permute-start | bytes 786440 | tf_op jit(solution)/shard_map/ppermute | solution.py:203
  14.1 2.1 %serve_rows.9 = f32[128,2048]{1,0:T(8,128)S(1)} custom-call(bf16[1024,128]{1,0:T(8,128)(2,1)S(1)} %collective-permute-done.2.refs_0_, bf16[1056,128]{1,0:T(8,128)(2,1)S(1)} %collective-permute-done.4.refs_1_, bf16[2048,768]{1,0:T(8,128)(2,1)S(1)} %get-tuple-element.22.refs_2_.refs_1_, bf16[2048,384]{1,0:T(8,128)(2,1)S(1)} %get-tuple-element.23.refs_3_.refs_2_, ...), custom_call_target="tpu_custom_call" | custom-call | tf_op jit(solution)/shard_map/serve_rows/pallas_call | solution.py:184
  16.2 1.6 %collective-permute-start.11 = (bf16[128,2048]{1,0:T(8,128)(2,1)S(1)}, bf16[128,2048]{1,0:T(8,128)(2,1)S(1)}, u32[]{:S(2)}, u32[]{:S(2)}) collective-permute-start(bf16[128,2048]{1,0:T(8,128)(2,1)S(1)} %convert_element_type.57), channel_id=1, source_target_pairs={{0,4},{1,3},{2,0},{3,7},{4,8},{5,1},{6,2},{7,11},{8,12},{9,5},{10,... | collective-permute-start | bytes 1572872 | tf_op jit(solution)/shard_map/ppermute | solution.py:219
  17.8 0.6 collective-permute-done.3.refs_0_
  18.5 2.2 %collective-permute-start.6 = (bf16[2080,128]{1,0:T(8,128)(2,1)S(1)}, bf16[2080,128]{1,0:T(8,128)(2,1)S(1)}, u32[]{:S(2)}, u32[]{:S(2)}) collective-permute-start(bf16[2080,128]{1,0:T(8,128)(2,1)S(1)} %pad_maximum_fusion), channel_id=1, source_target_pairs={{0,4},{1,3},{2,0},{3,7},{4,8},{5,1},{6,2},{7,11},{8,12},{9,5},{10,... | collective-permute-start | bytes 1597448 | tf_op jit(solution)/shard_map/ppermute | solution.py:203
  20.6 2.1 %serve_rows.10 = f32[128,2048]{1,0:T(8,128)S(1)} custom-call(bf16[1024,128]{1,0:T(8,128)(2,1)S(1)} %collective-permute-done.3.refs_0_, bf16[1056,128]{1,0:T(8,128)(2,1)S(1)} %collective-permute-done.5.refs_1_, bf16[2048,768]{1,0:T(8,128)(2,1)S(1)} %get-tuple-element.22.refs_2_.refs_1_, bf16[2048,384]{1,0:T(8,128)(2,1)S(1)} %get-tuple-element.23.refs_3_.refs_2_, ...), custom_call_target="tpu_custom_call" | custom-call | tf_op jit(solution)/shard_map/serve_rows/pallas_call | solution.py:184
  22.7 2.8 %collective-permute-done.11 = bf16[128,2048]{1,0:T(8,128)(2,1)S(1)} collective-permute-done((bf16[128,2048]{1,0:T(8,128)(2,1)S(1)}, bf16[128,2048]{1,0:T(8,128)(2,1)S(1)}, u32[]{:S(2)}, u32[]{:S(2)}) %collective-permute-start.11) | collective-permute-done | bytes 524320 | tf_op jit(solution)/shard_map/ppermute | solution.py:219
  25.4 0.1 add_convert_fusion.4
  25.6 1.6 %collective-permute-start.12 = (bf16[128,2048]{1,0:T(8,128)(2,1)S(1)}, bf16[128,2048]{1,0:T(8,128)(2,1)S(1)}, u32[]{:S(2)}, u32[]{:S(2)}) collective-permute-start(bf16[128,2048]{1,0:T(8,128)(2,1)S(1)} %add_convert_fusion.4), channel_id=1, source_target_pairs={{0,4},{1,3},{2,0},{3,7},{4,8},{5,1},{6,2},{7,11},{8,12},{9,5},{10,... | collective-permute-start | bytes 1572872 | tf_op jit(solution)/shard_map/ppermute | solution.py:219
  27.2 3.9 %collective-permute-done.6.refs_0_ = bf16[2080,128]{1,0:T(8,128)(2,1)S(1)} collective-permute-done((bf16[2080,128]{1,0:T(8,128)(2,1)S(1)}, bf16[2080,128]{1,0:T(8,128)(2,1)S(1)}, u32[]{:S(2)}, u32[]{:S(2)}) %collective-permute-start.6) | collective-permute-done | bytes 532512 | tf_op jit(solution)/shard_map/ppermute | solution.py:203
  31.2 1.6 %collective-permute-start.7 = (bf16[2080,128]{1,0:T(8,128)(2,1)S(1)}, bf16[2080,128]{1,0:T(8,128)(2,1)S(1)}, u32[]{:S(2)}, u32[]{:S(2)}) collective-permute-start(bf16[2080,128]{1,0:T(8,128)(2,1)S(1)} %collective-permute-done.6.refs_0_), channel_id=1, source_target_pairs={{0,4},{1,3},{2,0},{3,7},{4,8},{5,1},{6,2},{7,11},{8,12},{9,5},{10,... | collective-permute-start | bytes 1597448 | tf_op jit(solution)/shard_map/ppermute | solution.py:203
  32.7 2.0 %serve_rows.11 = f32[128,2048]{1,0:T(8,128)S(1)} custom-call(bf16[2080,128]{1,0:T(8,128)(2,1)S(1)} %collective-permute-done.6.refs_0_, bf16[2048,768]{1,0:T(8,128)(2,1)S(1)} %get-tuple-element.22.refs_2_.refs_1_, bf16[2048,384]{1,0:T(8,128)(2,1)S(1)} %get-tuple-element.23.refs_3_.refs_2_, bf16[2048,768]{1,0:T(8,128)(2,1)S(1)} %collective-permute-done.refs_4_.refs_3_, ...), custom_call_target="tpu_custom_call" | custom-call | tf_op jit(solution)/shard_map/serve_rows/pallas_call | solution.py:184
  34.7 2.0 %collective-permute-done.12 = bf16[128,2048]{1,0:T(8,128)(2,1)S(1)} collective-permute-done((bf16[128,2048]{1,0:T(8,128)(2,1)S(1)}, bf16[128,2048]{1,0:T(8,128)(2,1)S(1)}, u32[]{:S(2)}, u32[]{:S(2)}) %collective-permute-start.12) | collective-permute-done | bytes 524320 | tf_op jit(solution)/shard_map/ppermute | solution.py:219
  36.9 1.6 %collective-permute-start.13 = (bf16[128,2048]{1,0:T(8,128)(2,1)S(1)}, bf16[128,2048]{1,0:T(8,128)(2,1)S(1)}, u32[]{:S(2)}, u32[]{:S(2)}) collective-permute-start(bf16[128,2048]{1,0:T(8,128)(2,1)S(1)} %add_convert_fusion.3), channel_id=1, source_target_pairs={{0,4},{1,3},{2,0},{3,7},{4,8},{5,1},{6,2},{7,11},{8,12},{9,5},{10,... | collective-permute-start | bytes 1572872 | tf_op jit(solution)/shard_map/ppermute | solution.py:219
  38.5 4.0 %collective-permute-done.7.refs_0_ = bf16[2080,128]{1,0:T(8,128)(2,1)S(1)} collective-permute-done((bf16[2080,128]{1,0:T(8,128)(2,1)S(1)}, bf16[2080,128]{1,0:T(8,128)(2,1)S(1)}, u32[]{:S(2)}, u32[]{:S(2)}) %collective-permute-start.7) | collective-permute-done | bytes 532512 | tf_op jit(solution)/shard_map/ppermute | solution.py:203
  42.5 1.6 %collective-permute-start.8 = (bf16[2080,128]{1,0:T(8,128)(2,1)S(1)}, bf16[2080,128]{1,0:T(8,128)(2,1)S(1)}, u32[]{:S(2)}, u32[]{:S(2)}) collective-permute-start(bf16[2080,128]{1,0:T(8,128)(2,1)S(1)} %collective-permute-done.7.refs_0_), channel_id=1, source_target_pairs={{0,4},{1,3},{2,0},{3,7},{4,8},{5,1},{6,2},{7,11},{8,12},{9,5},{10,... | collective-permute-start | bytes 1597448 | tf_op jit(solution)/shard_map/ppermute | solution.py:203
  44.1 2.1 %serve_rows.12 = f32[128,2048]{1,0:T(8,128)S(1)} custom-call(bf16[2080,128]{1,0:T(8,128)(2,1)S(1)} %collective-permute-done.7.refs_0_, bf16[2048,768]{1,0:T(8,128)(2,1)S(1)} %get-tuple-element.22.refs_2_.refs_1_, bf16[2048,384]{1,0:T(8,128)(2,1)S(1)} %get-tuple-element.23.refs_3_.refs_2_, bf16[2048,768]{1,0:T(8,128)(2,1)S(1)} %collective-permute-done.refs_4_.refs_3_, ...), custom_call_target="tpu_custom_call" | custom-call | tf_op jit(solution)/shard_map/serve_rows/pallas_call | solution.py:184
  46.1 2.0 %collective-permute-done.13 = bf16[128,2048]{1,0:T(8,128)(2,1)S(1)} collective-permute-done((bf16[128,2048]{1,0:T(8,128)(2,1)S(1)}, bf16[128,2048]{1,0:T(8,128)(2,1)S(1)}, u32[]{:S(2)}, u32[]{:S(2)}) %collective-permute-start.13) | collective-permute-done | bytes 524320 | tf_op jit(solution)/shard_map/ppermute | solution.py:219
  48.2 1.6 %collective-permute-start.14 = (bf16[128,2048]{1,0:T(8,128)(2,1)S(1)}, bf16[128,2048]{1,0:T(8,128)(2,1)S(1)}, u32[]{:S(2)}, u32[]{:S(2)}) collective-permute-start(bf16[128,2048]{1,0:T(8,128)(2,1)S(1)} %add_convert_fusion.2), channel_id=1, source_target_pairs={{0,4},{1,3},{2,0},{3,7},{4,8},{5,1},{6,2},{7,11},{8,12},{9,5},{10,... | collective-permute-start | bytes 1572872 | tf_op jit(solution)/shard_map/ppermute | solution.py:219
  49.8 4.0 %collective-permute-done.8.refs_0_ = bf16[2080,128]{1,0:T(8,128)(2,1)S(1)} collective-permute-done((bf16[2080,128]{1,0:T(8,128)(2,1)S(1)}, bf16[2080,128]{1,0:T(8,128)(2,1)S(1)}, u32[]{:S(2)}, u32[]{:S(2)}) %collective-permute-start.8) | collective-permute-done | bytes 532512 | tf_op jit(solution)/shard_map/ppermute | solution.py:203
  53.8 1.6 %collective-permute-start.9 = (bf16[2080,128]{1,0:T(8,128)(2,1)S(1)}, bf16[2080,128]{1,0:T(8,128)(2,1)S(1)}, u32[]{:S(2)}, u32[]{:S(2)}) collective-permute-start(bf16[2080,128]{1,0:T(8,128)(2,1)S(1)} %collective-permute-done.8.refs_0_), channel_id=1, source_target_pairs={{0,4},{1,3},{2,0},{3,7},{4,8},{5,1},{6,2},{7,11},{8,12},{9,5},{10,... | collective-permute-start | bytes 1597448 | tf_op jit(solution)/shard_map/ppermute | solution.py:203
  55.4 2.0 %serve_rows.13 = f32[128,2048]{1,0:T(8,128)S(1)} custom-call(bf16[2080,128]{1,0:T(8,128)(2,1)S(1)} %collective-permute-done.8.refs_0_, bf16[2048,768]{1,0:T(8,128)(2,1)S(1)} %get-tuple-element.22.refs_2_.refs_1_, bf16[2048,384]{1,0:T(8,128)(2,1)S(1)} %get-tuple-element.23.refs_3_.refs_2_, bf16[2048,768]{1,0:T(8,128)(2,1)S(1)} %collective-permute-done.refs_4_.refs_3_, ...), custom_call_target="tpu_custom_call" | custom-call | tf_op jit(solution)/shard_map/serve_rows/pallas_call | solution.py:184
  57.4 2.0 %collective-permute-done.14 = bf16[128,2048]{1,0:T(8,128)(2,1)S(1)} collective-permute-done((bf16[128,2048]{1,0:T(8,128)(2,1)S(1)}, bf16[128,2048]{1,0:T(8,128)(2,1)S(1)}, u32[]{:S(2)}, u32[]{:S(2)}) %collective-permute-start.14) | collective-permute-done | bytes 524320 | tf_op jit(solution)/shard_map/ppermute | solution.py:219
  59.5 1.6 %collective-permute-start.15 = (bf16[128,2048]{1,0:T(8,128)(2,1)S(1)}, bf16[128,2048]{1,0:T(8,128)(2,1)S(1)}, u32[]{:S(2)}, u32[]{:S(2)}) collective-permute-start(bf16[128,2048]{1,0:T(8,128)(2,1)S(1)} %add_convert_fusion.1), channel_id=1, source_target_pairs={{0,4},{1,3},{2,0},{3,7},{4,8},{5,1},{6,2},{7,11},{8,12},{9,5},{10,... | collective-permute-start | bytes 1572872 | tf_op jit(solution)/shard_map/ppermute | solution.py:219
  61.2 4.0 %collective-permute-done.9.refs_0_ = bf16[2080,128]{1,0:T(8,128)(2,1)S(1)} collective-permute-done((bf16[2080,128]{1,0:T(8,128)(2,1)S(1)}, bf16[2080,128]{1,0:T(8,128)(2,1)S(1)}, u32[]{:S(2)}, u32[]{:S(2)}) %collective-permute-start.9) | collective-permute-done | bytes 532512 | tf_op jit(solution)/shard_map/ppermute | solution.py:203
  65.1 1.6 %collective-permute-start.10 = (bf16[2080,128]{1,0:T(8,128)(2,1)S(1)}, bf16[2080,128]{1,0:T(8,128)(2,1)S(1)}, u32[]{:S(2)}, u32[]{:S(2)}) collective-permute-start(bf16[2080,128]{1,0:T(8,128)(2,1)S(1)} %collective-permute-done.9.refs_0_), channel_id=1, source_target_pairs={{0,4},{1,3},{2,0},{3,7},{4,8},{5,1},{6,2},{7,11},{8,12},{9,5},{10,... | collective-permute-start | bytes 1597448 | tf_op jit(solution)/shard_map/ppermute | solution.py:203
  66.7 2.0 %serve_rows.14 = f32[128,2048]{1,0:T(8,128)S(1)} custom-call(bf16[2080,128]{1,0:T(8,128)(2,1)S(1)} %collective-permute-done.9.refs_0_, bf16[2048,768]{1,0:T(8,128)(2,1)S(1)} %get-tuple-element.22.refs_2_.refs_1_, bf16[2048,384]{1,0:T(8,128)(2,1)S(1)} %get-tuple-element.23.refs_3_.refs_2_, bf16[2048,768]{1,0:T(8,128)(2,1)S(1)} %collective-permute-done.refs_4_.refs_3_, ...), custom_call_target="tpu_custom_call" | custom-call | tf_op jit(solution)/shard_map/serve_rows/pallas_call | solution.py:184
  68.7 2.0 %collective-permute-done.15 = bf16[128,2048]{1,0:T(8,128)(2,1)S(1)} collective-permute-done((bf16[128,2048]{1,0:T(8,128)(2,1)S(1)}, bf16[128,2048]{1,0:T(8,128)(2,1)S(1)}, u32[]{:S(2)}, u32[]{:S(2)}) %collective-permute-start.15) | collective-permute-done | bytes 524320 | tf_op jit(solution)/shard_map/ppermute | solution.py:219
  70.9 1.6 %collective-permute-start.16 = (bf16[64,2048]{1,0:T(8,128)(2,1)S(1)}, bf16[64,2048]{1,0:T(8,128)(2,1)S(1)}, u32[]{:S(2)}, u32[]{:S(2)}) collective-permute-start(bf16[64,2048]{1,0:T(8,128)(2,1)S(1)} %fusion.2), channel_id=1, source_target_pairs={{0,4},{1,3},{2,0},{3,7},{4,8},{5,1},{6,2},{7,11},{8,12},{9,5},{10,... | collective-permute-start | bytes 786440 | tf_op jit(solution)/shard_map/ppermute | solution.py:219
  72.5 1.8 %collective-permute-start.18 = (bf16[64,2048]{1,0:T(8,128)(2,1)S(1)}, bf16[64,2048]{1,0:T(8,128)(2,1)S(1)}, u32[]{:S(2)}, u32[]{:S(2)}) collective-permute-start(bf16[64,2048]{1,0:T(8,128)(2,1)S(1)} %fusion), channel_id=1, source_target_pairs={{0,4},{1,3},{2,0},{3,7},{4,8},{5,1},{6,2},{7,11},{8,12},{9,5},{10,... | collective-permute-start | bytes 786440 | tf_op jit(solution)/shard_map/ppermute | solution.py:219
  74.4 2.1 %collective-permute-done.10.refs_0_ = bf16[2080,128]{1,0:T(8,128)(2,1)S(1)} collective-permute-done((bf16[2080,128]{1,0:T(8,128)(2,1)S(1)}, bf16[2080,128]{1,0:T(8,128)(2,1)S(1)}, u32[]{:S(2)}, u32[]{:S(2)}) %collective-permute-start.10) | collective-permute-done | bytes 532512 | tf_op jit(solution)/shard_map/ppermute | solution.py:203
  76.4 2.0 %serve_rows.15 = f32[128,2048]{1,0:T(8,128)S(1)} custom-call(bf16[2080,128]{1,0:T(8,128)(2,1)S(1)} %collective-permute-done.10.refs_0_, bf16[2048,768]{1,0:T(8,128)(2,1)S(1)} %get-tuple-element.22.refs_2_.refs_1_, bf16[2048,384]{1,0:T(8,128)(2,1)S(1)} %get-tuple-element.23.refs_3_.refs_2_, bf16[2048,768]{1,0:T(8,128)(2,1)S(1)} %collective-permute-done.refs_4_.refs_3_, ...), custom_call_target="tpu_custom_call" | custom-call | tf_op jit(solution)/shard_map/serve_rows/pallas_call | solution.py:184
  78.5 0.8 collective-permute-done.16
  79.3 2.7 %collective-permute-done.18 = bf16[64,2048]{1,0:T(8,128)(2,1)S(1)} collective-permute-done((bf16[64,2048]{1,0:T(8,128)(2,1)S(1)}, bf16[64,2048]{1,0:T(8,128)(2,1)S(1)}, u32[]{:S(2)}, u32[]{:S(2)}) %collective-permute-start.18) | collective-permute-done | bytes 262176 | tf_op jit(solution)/shard_map/ppermute | solution.py:219
  82.1 1.6 %collective-permute-start.19 = (bf16[64,2048]{1,0:T(8,128)(2,1)S(1)}, bf16[64,2048]{1,0:T(8,128)(2,1)S(1)}, u32[]{:S(2)}, u32[]{:S(2)}) collective-permute-start(bf16[64,2048]{1,0:T(8,128)(2,1)S(1)} %fusion.1), channel_id=1, source_target_pairs={{0,4},{1,3},{2,0},{3,7},{4,8},{5,1},{6,2},{7,11},{8,12},{9,5},{10,... | collective-permute-start | bytes 786440 | tf_op jit(solution)/shard_map/ppermute | solution.py:219
  83.8 1.6 %collective-permute-start.17 = (bf16[64,2048]{1,0:T(8,128)(2,1)S(1)}, bf16[64,2048]{1,0:T(8,128)(2,1)S(1)}, u32[]{:S(2)}, u32[]{:S(2)}) collective-permute-start(bf16[64,2048]{1,0:T(8,128)(2,1)S(1)} %fusion.3), channel_id=1, source_target_pairs={{0,4},{1,3},{2,0},{3,7},{4,8},{5,1},{6,2},{7,11},{8,12},{9,5},{10,... | collective-permute-start | bytes 786440 | tf_op jit(solution)/shard_map/ppermute | solution.py:219
  85.3 2.0 %serve_rows.8 = f32[128,2048]{1,0:T(8,128)S(1)} custom-call(bf16[1024,128]{1,0:T(8,128)(2,1)S(1)} %get-tuple-element.20.refs_0_, bf16[1056,128]{1,0:T(8,128)(2,1)S(1)} %get-tuple-element.21.refs_1_, bf16[2048,768]{1,0:T(8,128)(2,1)S(1)} %get-tuple-element.22.refs_2_.refs_1_, bf16[2048,384]{1,0:T(8,128)(2,1)S(1)} %get-tuple-element.23.refs_3_.refs_2_, ...), custom_call_target="tpu_custom_call" | custom-call | tf_op jit(solution)/shard_map/serve_rows/pallas_call | solution.py:184
  87.4 1.2 %collective-permute-done.19 = bf16[64,2048]{1,0:T(8,128)(2,1)S(1)} collective-permute-done((bf16[64,2048]{1,0:T(8,128)(2,1)S(1)}, bf16[64,2048]{1,0:T(8,128)(2,1)S(1)}, u32[]{:S(2)}, u32[]{:S(2)}) %collective-permute-start.19) | collective-permute-done | bytes 262176 | tf_op jit(solution)/shard_map/ppermute | solution.py:219
  88.5 2.8 %collective-permute-done.17 = bf16[64,2048]{1,0:T(8,128)(2,1)S(1)} collective-permute-done((bf16[64,2048]{1,0:T(8,128)(2,1)S(1)}, bf16[64,2048]{1,0:T(8,128)(2,1)S(1)}, u32[]{:S(2)}, u32[]{:S(2)}) %collective-permute-start.17) | collective-permute-done | bytes 262176 | tf_op jit(solution)/shard_map/ppermute | solution.py:219
  91.4 0.9 add_convert_fusion
  (14 shorter events, 0.7 us)
Async XLA Ops:
  0.0 14.1 %collective-permute-start = (bf16[2048,768]{1,0:T(8,128)(2,1)}, bf16[2048,768]{1,0:T(8,128)(2,1)S(1)}, u32[]{:S(2)}, u32[]{:S(2)}) collective-permute-start(bf16[2048,768]{1,0:T(8,128)(2,1)} %bitcast.4), channel_id=1, source_target_pairs={{0,1},{1,0},{2,3},{3,2},{4,5},{5,4},{6,7},{7,6},{8,9},{9,8},{10,11... | collective-permute-start | bytes 9437192 | tf_op jit(solution)/shard_map/ppermute | solution.py:171
  0.5 13.6 %collective-permute-start.1 = (bf16[2048,384]{1,0:T(8,128)(2,1)}, bf16[2048,384]{1,0:T(8,128)(2,1)S(1)}, u32[]{:S(2)}, u32[]{:S(2)}) collective-permute-start(bf16[2048,384]{1,0:T(8,128)(2,1)} %bitcast.6), channel_id=1, source_target_pairs={{0,1},{1,0},{2,3},{3,2},{4,5},{5,4},{6,7},{7,6},{8,9},{9,8},{10,11... | collective-permute-start | bytes 4718600 | tf_op jit(solution)/shard_map/ppermute | solution.py:171
  1.7 7.5 %collective-permute-start.4 = (bf16[1056,128]{1,0:T(8,128)(2,1)S(1)}, bf16[1056,128]{1,0:T(8,128)(2,1)S(1)}, u32[]{:S(2)}, u32[]{:S(2)}) collective-permute-start(bf16[1056,128]{1,0:T(8,128)(2,1)S(1)} %get-tuple-element.21.refs_1_), channel_id=1, source_target_pairs={{0,4},{1,3},{2,0},{3,7},{4,8},{5,1},{6,2},{7,11},{8,12},{9,5},{10,... | collective-permute-start | bytes 811016 | tf_op jit(solution)/shard_map/ppermute | solution.py:169
  4.8 7.2 %collective-permute-start.2 = (bf16[1024,128]{1,0:T(8,128)(2,1)S(1)}, bf16[1024,128]{1,0:T(8,128)(2,1)S(1)}, u32[]{:S(2)}, u32[]{:S(2)}) collective-permute-start(bf16[1024,128]{1,0:T(8,128)(2,1)S(1)} %get-tuple-element.20.refs_0_), channel_id=1, source_target_pairs={{0,4},{1,3},{2,0},{3,7},{4,8},{5,1},{6,2},{7,11},{8,12},{9,5},{10,... | collective-permute-start | bytes 786440 | tf_op jit(solution)/shard_map/ppermute | solution.py:169
  9.2 8.7 %collective-permute-start.5 = (bf16[1056,128]{1,0:T(8,128)(2,1)S(1)}, bf16[1056,128]{1,0:T(8,128)(2,1)S(1)}, u32[]{:S(2)}, u32[]{:S(2)}) collective-permute-start(bf16[1056,128]{1,0:T(8,128)(2,1)S(1)} %collective-permute-done.4.refs_1_), channel_id=1, source_target_pairs={{0,4},{1,3},{2,0},{3,7},{4,8},{5,1},{6,2},{7,11},{8,12},{9,5},{10,... | collective-permute-start | bytes 811016 | tf_op jit(solution)/shard_map/ppermute | solution.py:203
  12.0 6.5 %collective-permute-start.3 = (bf16[1024,128]{1,0:T(8,128)(2,1)S(1)}, bf16[1024,128]{1,0:T(8,128)(2,1)S(1)}, u32[]{:S(2)}, u32[]{:S(2)}) collective-permute-start(bf16[1024,128]{1,0:T(8,128)(2,1)S(1)} %collective-permute-done.2.refs_0_), channel_id=1, source_target_pairs={{0,4},{1,3},{2,0},{3,7},{4,8},{5,1},{6,2},{7,11},{8,12},{9,5},{10,... | collective-permute-start | bytes 786440 | tf_op jit(solution)/shard_map/ppermute | solution.py:203
  16.2 9.2 %collective-permute-start.11 = (bf16[128,2048]{1,0:T(8,128)(2,1)S(1)}, bf16[128,2048]{1,0:T(8,128)(2,1)S(1)}, u32[]{:S(2)}, u32[]{:S(2)}) collective-permute-start(bf16[128,2048]{1,0:T(8,128)(2,1)S(1)} %convert_element_type.57), channel_id=1, source_target_pairs={{0,4},{1,3},{2,0},{3,7},{4,8},{5,1},{6,2},{7,11},{8,12},{9,5},{10,... | collective-permute-start | bytes 1572872 | tf_op jit(solution)/shard_map/ppermute | solution.py:219
  18.5 12.7 %collective-permute-start.6 = (bf16[2080,128]{1,0:T(8,128)(2,1)S(1)}, bf16[2080,128]{1,0:T(8,128)(2,1)S(1)}, u32[]{:S(2)}, u32[]{:S(2)}) collective-permute-start(bf16[2080,128]{1,0:T(8,128)(2,1)S(1)} %pad_maximum_fusion), channel_id=1, source_target_pairs={{0,4},{1,3},{2,0},{3,7},{4,8},{5,1},{6,2},{7,11},{8,12},{9,5},{10,... | collective-permute-start | bytes 1597448 | tf_op jit(solution)/shard_map/ppermute | solution.py:203
  25.6 11.2 %collective-permute-start.12 = (bf16[128,2048]{1,0:T(8,128)(2,1)S(1)}, bf16[128,2048]{1,0:T(8,128)(2,1)S(1)}, u32[]{:S(2)}, u32[]{:S(2)}) collective-permute-start(bf16[128,2048]{1,0:T(8,128)(2,1)S(1)} %add_convert_fusion.4), channel_id=1, source_target_pairs={{0,4},{1,3},{2,0},{3,7},{4,8},{5,1},{6,2},{7,11},{8,12},{9,5},{10,... | collective-permute-start | bytes 1572872 | tf_op jit(solution)/shard_map/ppermute | solution.py:219
  31.2 11.3 %collective-permute-start.7 = (bf16[2080,128]{1,0:T(8,128)(2,1)S(1)}, bf16[2080,128]{1,0:T(8,128)(2,1)S(1)}, u32[]{:S(2)}, u32[]{:S(2)}) collective-permute-start(bf16[2080,128]{1,0:T(8,128)(2,1)S(1)} %collective-permute-done.6.refs_0_), channel_id=1, source_target_pairs={{0,4},{1,3},{2,0},{3,7},{4,8},{5,1},{6,2},{7,11},{8,12},{9,5},{10,... | collective-permute-start | bytes 1597448 | tf_op jit(solution)/shard_map/ppermute | solution.py:203
  36.9 11.2 %collective-permute-start.13 = (bf16[128,2048]{1,0:T(8,128)(2,1)S(1)}, bf16[128,2048]{1,0:T(8,128)(2,1)S(1)}, u32[]{:S(2)}, u32[]{:S(2)}) collective-permute-start(bf16[128,2048]{1,0:T(8,128)(2,1)S(1)} %add_convert_fusion.3), channel_id=1, source_target_pairs={{0,4},{1,3},{2,0},{3,7},{4,8},{5,1},{6,2},{7,11},{8,12},{9,5},{10,... | collective-permute-start | bytes 1572872 | tf_op jit(solution)/shard_map/ppermute | solution.py:219
  42.5 11.3 %collective-permute-start.8 = (bf16[2080,128]{1,0:T(8,128)(2,1)S(1)}, bf16[2080,128]{1,0:T(8,128)(2,1)S(1)}, u32[]{:S(2)}, u32[]{:S(2)}) collective-permute-start(bf16[2080,128]{1,0:T(8,128)(2,1)S(1)} %collective-permute-done.7.refs_0_), channel_id=1, source_target_pairs={{0,4},{1,3},{2,0},{3,7},{4,8},{5,1},{6,2},{7,11},{8,12},{9,5},{10,... | collective-permute-start | bytes 1597448 | tf_op jit(solution)/shard_map/ppermute | solution.py:203
  48.2 11.2 %collective-permute-start.14 = (bf16[128,2048]{1,0:T(8,128)(2,1)S(1)}, bf16[128,2048]{1,0:T(8,128)(2,1)S(1)}, u32[]{:S(2)}, u32[]{:S(2)}) collective-permute-start(bf16[128,2048]{1,0:T(8,128)(2,1)S(1)} %add_convert_fusion.2), channel_id=1, source_target_pairs={{0,4},{1,3},{2,0},{3,7},{4,8},{5,1},{6,2},{7,11},{8,12},{9,5},{10,... | collective-permute-start | bytes 1572872 | tf_op jit(solution)/shard_map/ppermute | solution.py:219
  53.8 11.3 %collective-permute-start.9 = (bf16[2080,128]{1,0:T(8,128)(2,1)S(1)}, bf16[2080,128]{1,0:T(8,128)(2,1)S(1)}, u32[]{:S(2)}, u32[]{:S(2)}) collective-permute-start(bf16[2080,128]{1,0:T(8,128)(2,1)S(1)} %collective-permute-done.8.refs_0_), channel_id=1, source_target_pairs={{0,4},{1,3},{2,0},{3,7},{4,8},{5,1},{6,2},{7,11},{8,12},{9,5},{10,... | collective-permute-start | bytes 1597448 | tf_op jit(solution)/shard_map/ppermute | solution.py:203
  59.5 11.2 %collective-permute-start.15 = (bf16[128,2048]{1,0:T(8,128)(2,1)S(1)}, bf16[128,2048]{1,0:T(8,128)(2,1)S(1)}, u32[]{:S(2)}, u32[]{:S(2)}) collective-permute-start(bf16[128,2048]{1,0:T(8,128)(2,1)S(1)} %add_convert_fusion.1), channel_id=1, source_target_pairs={{0,4},{1,3},{2,0},{3,7},{4,8},{5,1},{6,2},{7,11},{8,12},{9,5},{10,... | collective-permute-start | bytes 1572872 | tf_op jit(solution)/shard_map/ppermute | solution.py:219
  65.1 11.3 %collective-permute-start.10 = (bf16[2080,128]{1,0:T(8,128)(2,1)S(1)}, bf16[2080,128]{1,0:T(8,128)(2,1)S(1)}, u32[]{:S(2)}, u32[]{:S(2)}) collective-permute-start(bf16[2080,128]{1,0:T(8,128)(2,1)S(1)} %collective-permute-done.9.refs_0_), channel_id=1, source_target_pairs={{0,4},{1,3},{2,0},{3,7},{4,8},{5,1},{6,2},{7,11},{8,12},{9,5},{10,... | collective-permute-start | bytes 1597448 | tf_op jit(solution)/shard_map/ppermute | solution.py:203
  70.9 8.4 %collective-permute-start.16 = (bf16[64,2048]{1,0:T(8,128)(2,1)S(1)}, bf16[64,2048]{1,0:T(8,128)(2,1)S(1)}, u32[]{:S(2)}, u32[]{:S(2)}) collective-permute-start(bf16[64,2048]{1,0:T(8,128)(2,1)S(1)} %fusion.2), channel_id=1, source_target_pairs={{0,4},{1,3},{2,0},{3,7},{4,8},{5,1},{6,2},{7,11},{8,12},{9,5},{10,... | collective-permute-start | bytes 786440 | tf_op jit(solution)/shard_map/ppermute | solution.py:219
  72.5 9.5 %collective-permute-start.18 = (bf16[64,2048]{1,0:T(8,128)(2,1)S(1)}, bf16[64,2048]{1,0:T(8,128)(2,1)S(1)}, u32[]{:S(2)}, u32[]{:S(2)}) collective-permute-start(bf16[64,2048]{1,0:T(8,128)(2,1)S(1)} %fusion), channel_id=1, source_target_pairs={{0,4},{1,3},{2,0},{3,7},{4,8},{5,1},{6,2},{7,11},{8,12},{9,5},{10,... | collective-permute-start | bytes 786440 | tf_op jit(solution)/shard_map/ppermute | solution.py:219
  82.1 6.4 %collective-permute-start.19 = (bf16[64,2048]{1,0:T(8,128)(2,1)S(1)}, bf16[64,2048]{1,0:T(8,128)(2,1)S(1)}, u32[]{:S(2)}, u32[]{:S(2)}) collective-permute-start(bf16[64,2048]{1,0:T(8,128)(2,1)S(1)} %fusion.1), channel_id=1, source_target_pairs={{0,4},{1,3},{2,0},{3,7},{4,8},{5,1},{6,2},{7,11},{8,12},{9,5},{10,... | collective-permute-start | bytes 786440 | tf_op jit(solution)/shard_map/ppermute | solution.py:219
  83.8 7.6 %collective-permute-start.17 = (bf16[64,2048]{1,0:T(8,128)(2,1)S(1)}, bf16[64,2048]{1,0:T(8,128)(2,1)S(1)}, u32[]{:S(2)}, u32[]{:S(2)}) collective-permute-start(bf16[64,2048]{1,0:T(8,128)(2,1)S(1)} %fusion.3), channel_id=1, source_target_pairs={{0,4},{1,3},{2,0},{3,7},{4,8},{5,1},{6,2},{7,11},{8,12},{9,5},{10,... | collective-permute-start | bytes 786440 | tf_op jit(solution)/shard_map/ppermute | solution.py:219
